TPU v7x, 32 devices: a whole 2x2x4 slice. The times are simulated.
32 devices in a mesh: row: 8 (over z, x), col: 4 (over y, core).
Axes of the slice: x: 2, y: 2, z: 4, core: 2. Of those that a mesh axis runs over, the one named last changes fastest.
Arguments:
- trailing: float32 [8192, 1536], P('row', 'col'), may hold values from -6 to 6
- reflectors: float32 [8192, 256], P('row', 'col'), may hold values from -6 to 6
- factor: float32 [256, 256], replicated, as said below
- column_sums: float32 [8192, 8], P('row', 'col'), may hold values from -6 to 6
- row_sums: float32 [16, 1536], P('row', 'col'), may hold values from -6 to 6
Outputs:
- updated: float32 [8192, 1536], P('row', 'col')
- column_checks: float32 [8192, 8], P('row', 'col')
- row_checks: float32 [16, 1536], P('row', 'col')
Inputs may be any that keep to these rules, and one draw needn't show every extreme that they name: `factor`: zero below the diagonal.
All inputs are finite; a program needn't handle non-finite values.
Results may differ from a plain program's by a relative error of at most 0.000067.
Values sent between devices are 32-bit elements; how exact they have to be, the bound alone decides.
No kernel may reach another device: no remote copies, remote signals or barrier semaphores. Data moves between devices by JAX's collectives and lax.ppermute only.
A program may use at most 64 MiB of HBM per device.

v0:
```python
import jax
import jax.numpy as jnp
from jax import lax
from jax.sharding import PartitionSpec as P


def matmul(left, right):
    return jnp.dot(left, right, precision=lax.Precision.HIGHEST, preferred_element_type=jnp.float32)


def shards(trailing, reflectors, factor, column_sums, row_sums):
    panel = lax.all_gather(reflectors, "col", axis=1, tiled=True)
    columns = trailing.shape[1]
    joined = jnp.concatenate([trailing, column_sums], axis=1)
    product = matmul(panel.T, joined)
    product_main = product[:, :columns]
    product_check = product[:, columns:]
    summed_main, summed_check = lax.psum((product_main, product_check), "row")
    main_image = matmul(factor.T, summed_main)
    check_image = matmul(factor.T, summed_check)
    updated = trailing - matmul(panel, main_image)
    column_checks = column_sums - matmul(panel, check_image)
    count = trailing.shape[0]
    local = jnp.arange(count).astype(jnp.float32)
    scale = 1.0 / jnp.sqrt(jnp.float32(count))
    weights = jnp.stack([jnp.ones((count,), jnp.float32) * scale, (local + 1.0) * scale / count])
    check_coeff = matmul(weights, panel)
    row_checks = row_sums - matmul(check_coeff, main_image)
    return (updated, column_checks, row_checks)


def solution(mesh):
    placed = (P("row", "col"), P("row", "col"), P(), P("row", "col"), P("row", "col"))
    return jax.shard_map(
        shards,
        mesh=mesh,
        in_specs=placed,
        out_specs=(P("row", "col"), P("row", "col"), P("row", "col")),
        check_vma=False,
    )
```

profile of v0, /device:TPU:0, one launch (start us, length us, event | category | flops | bytes accessed | tf_op | source)
XLA Modules:
  0.0 139.2 jit_solution(17977182560160107712)
XLA Ops:
  7.2 0.0 copy-start
  7.2 0.0 all-gather.2.cloned.1.call-start
  7.2 0.7 all-gather.2.cloned.1.call-update
  7.9 0.0 all-reduce.3.cloned.1.call-start
  8.0 0.9 copy.8
  8.9 0.0 copy-start.2
  8.9 3.1 %copy.9 = f32[1024,384]{0,1:T(8,128)} copy(f32[1024,384]{1,0:T(8,128)} %param.5) | data formatting | bytes 3145728 | tf_op args[0]
  12.0 17.0 %all-gather.2.cloned.1.call-done = f32[1024,256]{0,1:T(8,128)} async-done(((f32[1024,64]{0,1:T(8,128)}), f32[1024,256]{0,1:T(8,128)}) %all-gather.2.cloned.1.call-update) | async-done | bytes 1048592 | tf_op jit(solution)/shard_map/all_gather | solution.py:12
  29.0 0.0 copy-done.2
  29.0 0.0 copy-start.1
  29.0 4.7 %fusion.4 = f32[256,386]{0,1:T(8,128)S(1)} fusion(f32[1024,256]{0,1:T(8,128)} %all-gather.2.cloned.1.call-done, f32[1024,2]{1,0:T(8,128)S(1)} %copy.8, f32[1024,384]{1,0:T(8,128)S(1)} %copy-done.2), kind=kOutput, calls=%fused_computation.5 | convolution fusion | flops 1214646272 | bytes 3024896 | tf_op jit(solution)/shard_map/dot_general | solution.py:8
  33.8 0.0 copy-start.4
  33.8 0.8 slice.8
  34.5 21.3 %psum.15 = f32[256,2]{0,1:T(2,128)S(1)} all-reduce(f32[256,2]{0,1:T(2,128)S(1)} %slice.9), channel_id=1, replica_groups=mesh['row'=8,'col'=4] {'row'}, use_global_device_ids=true, to_apply=%region_1.0 | all-reduce | flops 512 | bytes 4096 | tf_op jit(solution)/shard_map/psum | solution.py:18
  55.9 0.0 all-reduce.3.cloned.1.call-update
  55.9 0.0 copy-done.1
  55.9 0.0 copy-start.3
  55.9 0.9 fusion.8
  56.8 0.0 copy-done
  56.8 0.2 fusion.13
  57.0 0.0 copy-done.4
  57.1 1.2 fusion.7
  58.3 65.9 %all-reduce.3.cloned.1.call-done = f32[256,384]{0,1:T(8,128)} async-done(((f32[256,384]{0,1:T(8,128)}), f32[256,384]{0,1:T(8,128)}) %all-reduce.3.cloned.1.call-update) | async-done | bytes 393232 | tf_op jit(solution)/shard_map/psum | solution.py:18
  124.2 1.5 %fusion.12 = f32[384,256]{1,0:T(8,128)S(1)} fusion(f32[256,384]{0,1:T(8,128)} %all-reduce.3.cloned.1.call-done, f32[256,256]{1,0:T(8,128)S(1)} %copy-done), kind=kOutput, calls=%fused_computation.14 | convolution fusion | flops 301989888 | bytes 1048576 | tf_op jit(solution)/shard_map/dot_general | solution.py:8
  125.7 0.0 copy-done.3
  125.7 2.6 %bitcast_subtract_fusion = f32[1024,384]{0,1:T(8,128)} fusion(f32[1024,384]{0,1:T(8,128)S(1)} %copy-done.3, f32[384,256]{1,0:T(8,128)S(1)} %fusion.12, f32[1024,256]{0,1:T(8,128)S(1)} %copy-done.1), kind=kOutput, calls=%fused_computation.4 | convolution fusion | flops 1208352768 | bytes 4587520 | tf_op jit(solution)/shard_map/dot_general | solution.py:8
  128.3 0.0 copy-start.5
  128.3 3.0 %copy.10 = f32[1024,384]{1,0:T(8,128)} copy(f32[1024,384]{0,1:T(8,128)} %bitcast_subtract_fusion) | data formatting | bytes 3145728
  131.4 0.0 copy-done.5
  131.4 1.0 convolution_subtract_fusion
  (2 shorter events, 0.0 us)
Async XLA Ops:
  7.2 49.7 %copy-start = (f32[256,256]{1,0:T(8,128)S(1)}, f32[256,256]{1,0:T(8,128)}, u32[]{:S(2)}) copy-start(f32[256,256]{1,0:T(8,128)} %param.7) | copy-start | bytes 786436
  7.2 21.8 %all-gather.2.cloned.1.call-start = ((), (), s32[]{:S(2)}) async-start(), calls=%async_computation | async-start | bytes 1310720 | tf_op jit(solution)/shard_map/all_gather | solution.py:12
  7.9 116.3 %all-reduce.3.cloned.1.call-start = ((), (), s32[]{:S(2)}) async-start(), calls=%async_computation.1 | async-start | bytes 786432 | tf_op jit(solution)/shard_map/psum | solution.py:18
  8.9 20.1 %copy-start.2 = (f32[1024,384]{1,0:T(8,128)S(1)}, f32[1024,384]{1,0:T(8,128)}, u32[]{:S(2)}) copy-start(f32[1024,384]{1,0:T(8,128)} %param.5) | copy-start | bytes 4718596
  29.0 26.9 %copy-start.1 = (f32[1024,256]{0,1:T(8,128)S(1)}, f32[1024,256]{0,1:T(8,128)}, u32[]{:S(2)}) copy-start(f32[1024,256]{0,1:T(8,128)} %all-gather.2.cloned.1.call-done) | copy-start | bytes 3145732
  33.8 23.3 %copy-start.4 = (f32[1024,2]{0,1:T(2,128)S(1)}, f32[1024,2]{0,1:T(2,128)}, u32[]{:S(2)}) copy-start(f32[1024,2]{0,1:T(2,128)} %param.8) | copy-start | bytes 24580
  55.9 69.8 %copy-start.3 = (f32[1024,384]{0,1:T(8,128)S(1)}, f32[1024,384]{0,1:T(8,128)}, u32[]{:S(2)}) copy-start(f32[1024,384]{0,1:T(8,128)} %copy.9) | copy-start | bytes 4718596
  128.3 3.0 %copy-start.5 = (f32[2,384]{1,0:T(2,128)S(1)}, f32[2,384]{1,0:T(2,128)}, u32[]{:S(2)}) copy-start(f32[2,384]{1,0:T(2,128)} %param.9) | copy-start | bytes 9220
Sparse Core Ops, SparseCore 0:
  9.5 19.4 all-gather.1
  56.0 68.1 all-reduce.2
where the time goes:
time: 139 us
  waiting for transfers between devices  83.6 us (60%)
  blocking collectives  21.3 us (15%)
  between operations  14.1 us (10%)
  matrix products  12.2 us (9%)
  local copies, waits for them, and re-layouts  7.89 us (6%)
    psum x1, waiting for transfers between devices, shards(): summed_main, summed_check = lax.psum((product_main, product_check), 'row')  65.9 us
    psum x1, blocking collectives, shards(): summed_main, summed_check = lax.psum((product_main, product_check), 'row')  21.3 us
    all_gather x1, waiting for transfers between devices, shards(): panel = lax.all_gather(reflectors, 'col', axis=1, tiled=True)  17 us
    dot_general x7, matrix products, matmul(): jnp.dot(left, right, precision=lax.Precision.HIGHEST, preferred_element_t...  12.2 us
    unnamed x15, local copies, waits for them, and re-layouts  7.12 us
  transfers between devices with their start and end apart: 2, of which 2 were waited for; matrix products, arithmetic and copies ran while one was open for 5% of the time, Pallas kernels for 0%

commit v1 on v0

--- a/solution.py
+++ b/solution.py
@@ -9,7 +9,20 @@
 
 
 def shards(trailing, reflectors, factor, column_sums, row_sums):
-    panel = lax.all_gather(reflectors, "col", axis=1, tiled=True)
+
+    def _do_joints(point):
+        g_now, f_now, long_array = (lax.axis_size("col"), lax.axis_index("col"), point.shape[1])
+        inbox = [q * g_now if j0 == 1 else q for j0, q in enumerate(point.shape)]
+        upper = jnp.zeros(inbox, point.dtype)
+        response = lax.dynamic_update_slice_in_dim(upper, point, f_now * long_array, axis=1)
+        for ix in range(1, g_now):
+            point = lax.ppermute(point, "col", perm=[(j0, (j0 + 1) % g_now) for j0 in range(g_now)])
+            response = lax.dynamic_update_slice_in_dim(
+                response, point, (f_now - ix) % g_now * long_array, axis=1
+            )
+        return response
+
+    panel = _do_joints(reflectors)
     columns = trailing.shape[1]
     joined = jnp.concatenate([trailing, column_sums], axis=1)
     product = matmul(panel.T, joined)

time: 139 us -> 121 us (0.87)
  waiting for transfers between devices: 83.6 us -> 63.8 us
    all_gather x1 -> x0, waiting for transfers between devices: 17 us -> none  [shards(): panel = lax.all_gather(reflectors, 'col', axis=1, tiled=True)]
    psum x1, waiting for transfers between devices: 65.9 us -> 49.1 us  [shards(): summed_main, summed_check = lax.psum((product_main, product_check), 'row')]
    ppermute x0 -> x3, waiting for transfers between devices: none -> 14.7 us  [_do_joints(): lax.ppermute(point, 'col', perm=[(j0, (j0 + 1) % g_now) for j0 in range(g...]
    unnamed x15 -> x13, local copies, waits for them, and re-layouts: 7.12 us -> 0.99 us
    dynamic_update_slice x0 -> x4, local copies, waits for them, and re-layouts: none -> 4.01 us  [the longest x3 2.92 us: _do_joints(): lax.dynamic_update_slice_in_dim(response, point, (f_now - ix) % g_now * l...]
  transfers between devices with their start and end apart: 2 -> 4, of which waited for: 2 -> 4; matrix products, arithmetic and copies ran while one was open for 5% -> 5% of each run, Pallas kernels for 0% -> 0%
where the time goes in v1:
time: 121 us
  waiting for transfers between devices  63.8 us (53%)
  blocking collectives  22.5 us (19%)
  between operations  14.2 us (12%)
  matrix products  12.9 us (11%)
  local copies, waits for them, and re-layouts  6.59 us (5%)
    psum x1, waiting for transfers between devices, shards(): summed_main, summed_check = lax.psum((product_main, product_check), 'row')  49.1 us
    psum x1, blocking collectives, shards(): summed_main, summed_check = lax.psum((product_main, product_check), 'row')  22.5 us
    ppermute x3, waiting for transfers between devices, _do_joints(): lax.ppermute(point, 'col', perm=[(j0, (j0 + 1) % g_now) for j0 in range(g...  14.7 us
    dot_general x7, matrix products, matmul(): jnp.dot(left, right, precision=lax.Precision.HIGHEST, preferred_element_t...  12.9 us
    dynamic_update_slice x3, local copies, waits for them, and re-layouts, _do_joints(): lax.dynamic_update_slice_in_dim(response, point, (f_now - ix) % g_now * l...  2.92 us
  transfers between devices with their start and end apart: 4, of which 4 were waited for; matrix products, arithmetic and copies ran while one was open for 5% of the time, Pallas kernels for 0%

profile of v1, /device:TPU:0, one launch (start us, length us, event | category | flops | bytes accessed | tf_op | source)
XLA Modules:
  0.0 120.7 jit_solution(15927187103712420179)
XLA Ops:
  7.2 0.0 copy-start
  7.2 0.0 copy-start.4
  7.2 0.0 all-reduce.3.cloned.1.call-start
  7.2 0.5 collective-permute-start
  7.8 6.2 %collective-permute-done = f32[1024,64]{0,1:T(8,128)S(1)} collective-permute-done((f32[1024,64]{0,1:T(8,128)}, f32[1024,64]{0,1:T(8,128)S(1)}, u32[]{:S(2)}, u32[]{:S(2)}) %collective-permute-start) | collective-permute-done | bytes 262176 | tf_op jit(solution)/shard_map/ppermute | solution.py:19
  14.0 0.0 copy-start.3
  14.0 0.0 collective-permute-start.1
  14.0 0.1 broadcast_in_dim.3
  14.1 0.0 copy-start.1
  14.2 1.1 constant_dynamic-update-slice_fusion.3
  15.3 4.6 %collective-permute-done.1 = f32[1024,64]{0,1:T(8,128)} collective-permute-done((f32[1024,64]{0,1:T(8,128)S(1)}, f32[1024,64]{0,1:T(8,128)}, u32[]{:S(2)}, u32[]{:S(2)}) %collective-permute-start.1) | collective-permute-done | bytes 262176 | tf_op jit(solution)/shard_map/ppermute | solution.py:19
  19.9 0.0 collective-permute-start.2
  20.0 0.0 copy-done.3
  20.0 0.0 copy-done.4
  20.0 0.2 copy.8
  20.2 1.0 constant_dynamic-update-slice_fusion.2
  21.2 1.0 constant_dynamic-update-slice_fusion.1
  22.2 3.8 %collective-permute-done.2 = f32[1024,64]{0,1:T(8,128)} collective-permute-done((f32[1024,64]{0,1:T(8,128)}, f32[1024,64]{0,1:T(8,128)}, u32[]{:S(2)}, u32[]{:S(2)}) %collective-permute-start.2) | collective-permute-done | bytes 262176 | tf_op jit(solution)/shard_map/ppermute | solution.py:19
  26.0 1.0 constant_dynamic-update-slice_fusion
  27.0 0.0 copy-done.1
  27.0 3.4 %fusion = f32[256,386]{0,1:T(8,128)S(1)} fusion(f32[1024,256]{0,1:T(8,128)S(1)} %constant_dynamic-update-slice_fusion, f32[1024,2]{1,0:T(8,128)S(1)} %copy.8, f32[1024,384]{1,0:T(8,128)S(1)} %copy-done.1), kind=kOutput, calls=%fused_computation | convolution fusion | flops 1214646272 | bytes 3024896 | tf_op jit(solution)/shard_map/dot_general | solution.py:8
  30.4 0.0 copy-start.2
  30.5 0.7 copy-done.2
  31.2 0.8 slice.8
  32.0 0.7 slice.9
  32.7 0.0 all-reduce.3.cloned.1.call-update
  32.7 0.9 fusion.4
  33.6 22.5 %psum.15 = f32[256,2]{0,1:T(2,128)S(1)} all-reduce(f32[256,2]{0,1:T(2,128)S(1)} %slice.9), channel_id=1, replica_groups=mesh['row'=8,'col'=4] {'row'}, use_global_device_ids=true, to_apply=%region_1.2 | all-reduce | flops 512 | bytes 4096 | tf_op jit(solution)/shard_map/psum | solution.py:31
  56.1 0.0 copy-done
  56.1 0.2 fusion.9
  56.3 1.3 %convolution_subtract_fusion.1 = f32[1024,2]{0,1:T(2,128)} fusion(f32[1024,2]{0,1:T(2,128)S(1)} %copy-done.4, f32[1024,256]{0,1:T(8,128)S(1)} %constant_dynamic-update-slice_fusion, f32[2,256]{1,0:T(2,128)S(1)} %fusion.9), kind=kOutput, calls=%fused_computation.5 | convolution fusion | flops 6293504 | bytes 1067008 | tf_op jit(solution)/shard_map/dot_general | solution.py:8
  57.6 49.1 %all-reduce.3.cloned.1.call-done = f32[256,384]{0,1:T(8,128)} async-done(((f32[256,384]{0,1:T(8,128)}), f32[256,384]{0,1:T(8,128)}) %all-reduce.3.cloned.1.call-update) | async-done | bytes 393232 | tf_op jit(solution)/shard_map/psum | solution.py:31
  106.7 1.5 %fusion.8 = f32[384,256]{1,0:T(8,128)S(1)} fusion(f32[256,384]{0,1:T(8,128)} %all-reduce.3.cloned.1.call-done, f32[256,256]{1,0:T(8,128)S(1)} %copy-done), kind=kOutput, calls=%fused_computation.16 | convolution fusion | flops 301989888 | bytes 1048576 | tf_op jit(solution)/shard_map/dot_general | solution.py:8
  108.2 0.0 copy-start.5
  108.2 4.6 %convolution_subtract_fusion = f32[1024,384]{1,0:T(8,128)} fusion(f32[1024,384]{1,0:T(8,128)S(1)} %copy-done.1, f32[1024,256]{0,1:T(8,128)S(1)} %constant_dynamic-update-slice_fusion, f32[384,256]{1,0:T(8,128)S(1)} %fusion.8), kind=kOutput, calls=%fused_computation.4 | convolution fusion | flops 1208352768 | bytes 4587520 | tf_op jit(solution)/shard_map/dot_general | solution.py:8
  112.8 0.0 copy-done.5
  112.8 1.0 convolution_subtract_fusion.2
  (1 shorter events, 0.0 us)
Async XLA Ops:
  7.2 48.9 %copy-start = (f32[256,256]{1,0:T(8,128)S(1)}, f32[256,256]{1,0:T(8,128)}, u32[]{:S(2)}) copy-start(f32[256,256]{1,0:T(8,128)} %param.7) | copy-start | bytes 786436
  7.2 12.8 %copy-start.4 = (f32[1024,2]{0,1:T(2,128)S(1)}, f32[1024,2]{0,1:T(2,128)}, u32[]{:S(2)}) copy-start(f32[1024,2]{0,1:T(2,128)} %param.8) | copy-start | bytes 24580
  7.2 99.5 %all-reduce.3.cloned.1.call-start = ((), (), s32[]{:S(2)}) async-start(), calls=%async_computation | async-start | bytes 786432 | tf_op jit(solution)/shard_map/psum | solution.py:31
  7.2 6.8 %collective-permute-start = (f32[1024,64]{0,1:T(8,128)}, f32[1024,64]{0,1:T(8,128)S(1)}, u32[]{:S(2)}, u32[]{:S(2)}) collective-permute-start(f32[1024,64]{0,1:T(8,128)} %param.6), channel_id=1, source_target_pairs={{0,1},{1,2},{2,3},{3,0},{4,5},{5,6},{6,7},{7,4},{8,9},{9,10},{10,1... | collective-permute-start | bytes 786440 | tf_op jit(solution)/shard_map/ppermute | solution.py:19
  14.0 6.0 %copy-start.3 = (f32[1024,64]{0,1:T(8,128)}, f32[1024,64]{0,1:T(8,128)S(1)}, u32[]{:S(2)}) copy-start(f32[1024,64]{0,1:T(8,128)S(1)} %collective-permute-done) | copy-start | bytes 786436
  14.0 5.9 %collective-permute-start.1 = (f32[1024,64]{0,1:T(8,128)S(1)}, f32[1024,64]{0,1:T(8,128)}, u32[]{:S(2)}, u32[]{:S(2)}) collective-permute-start(f32[1024,64]{0,1:T(8,128)S(1)} %collective-permute-done), channel_id=1, source_target_pairs={{0,1},{1,2},{2,3},{3,0},{4,5},{5,6},{6,7},{7,4},{8,9},{9,10},{10,1... | collective-permute-start | bytes 786440 | tf_op jit(solution)/shard_map/ppermute | solution.py:19
  14.1 12.8 %copy-start.1 = (f32[1024,384]{1,0:T(8,128)S(1)}, f32[1024,384]{1,0:T(8,128)}, u32[]{:S(2)}) copy-start(f32[1024,384]{1,0:T(8,128)} %param.5) | copy-start | bytes 4718596
  19.9 6.1 %collective-permute-start.2 = (f32[1024,64]{0,1:T(8,128)}, f32[1024,64]{0,1:T(8,128)}, u32[]{:S(2)}, u32[]{:S(2)}) collective-permute-start(f32[1024,64]{0,1:T(8,128)} %collective-permute-done.1), channel_id=1, source_target_pairs={{0,1},{1,2},{2,3},{3,0},{4,5},{5,6},{6,7},{7,4},{8,9},{9,10},{10,1... | collective-permute-start | bytes 786440 | tf_op jit(solution)/shard_map/ppermute | solution.py:19
  30.4 0.8 copy-start.2
  108.2 4.6 %copy-start.5 = (f32[2,384]{1,0:T(2,128)S(1)}, f32[2,384]{1,0:T(2,128)}, u32[]{:S(2)}) copy-start(f32[2,384]{1,0:T(2,128)} %param.9) | copy-start | bytes 9220
Sparse Core Ops, SparseCore 0:
  32.8 73.8 all-reduce.2
